TPU v7x, 128 devices: a whole 4x4x4 slice. The times are simulated.
128 devices in a mesh: rows: 64 (over x, y_lo, z, core), rep: 2 (over y_hi).
Axes of the slice: x: 4, y: 4 (y_hi: 2, y_lo: 2; y = y_hi * 2 + y_lo), z: 4, core: 2. Of those that a mesh axis runs over, the one named last changes fastest.
Arguments:
- features: bfloat16 [65536, 128], P(('rows', 'rep')), may hold values from -6 to 6
- weight: bfloat16 [128, 256], replicated, may hold values from -0.5 to 0.5
- shift_bias: float32 [256], replicated, may hold values from -3 to 3
- norm_gain: float32 [256], replicated, may hold values from 0.25 to 1.75
- tile_values: bfloat16 [512, 2, 88, 128, 128], P('rows', 'rep'), as said below
- tile_cols: int32 [512, 2, 88], P('rows', 'rep'), may hold values from 0 to 255, all different within a row
- tile_counts: int32 [512, 2], P('rows', 'rep'), may hold values from 1 to 88, as said below
- block_order: int32 [2, 256], replicated, may hold values from 0 to 255, each once within a row
Outputs:
- node_out: bfloat16 [65536, 256], P(('rows', 'rep'))
Inputs may be any that keep to these rules, and one draw needn't show every extreme that they name: Slots 0 to tile_counts - 1 of a row block and column set are live, the rest are ignored; the largest count is reached. `tile_values`: tile entries are nonnegative.
All inputs are finite; a program needn't handle non-finite values.
Results may differ from a plain program's by a relative error of at most 0.0052.
Values may be sent and summed in bfloat16 or wider, within the bound.
No kernel may reach another device: no remote copies, remote signals or barrier semaphores. Data moves between devices by JAX's collectives and lax.ppermute only.
A program may use at most 192 MiB of HBM per device.

v0:
```python
import jax
import jax.numpy as jnp
from jax import lax
from jax.sharding import PartitionSpec as P


def per_device(
    features, weight, shift_bias, norm_gain, tile_values, tile_cols, tile_counts, block_order
):
    row_blocks = tile_values.shape[0]
    slot_count = tile_values.shape[2]
    block_size = tile_values.shape[3]
    hidden_width = weight.shape[1]
    projected = jnp.dot(features, weight, preferred_element_type=jnp.float32).astype(jnp.bfloat16)
    panel_rows = lax.all_gather(projected, "rows", axis=0, tiled=True)
    set_blocks = panel_rows.shape[0] // block_size
    panel_blocks = panel_rows.reshape(set_blocks, block_size, hidden_width)
    order_mine = lax.dynamic_index_in_dim(block_order, lax.axis_index("rep"), 0, keepdims=False)
    column_ids = tile_cols.reshape(row_blocks, slot_count)
    matches = column_ids[:, :, None] == jnp.arange(set_blocks, dtype=jnp.int32)[None, None, :]
    positions = jnp.sum(jnp.where(matches, order_mine[None, None, :], 0), axis=2)
    tile_block = tile_values.reshape(row_blocks, slot_count, block_size, block_size)
    live_count = tile_counts.reshape(row_blocks)
    picked_rows = panel_blocks[positions]
    live_mask = jnp.arange(slot_count, dtype=jnp.int32)[None, :] < live_count[:, None]
    picked_rows = jnp.where(live_mask[:, :, None, None], picked_rows, jnp.zeros((), jnp.bfloat16))
    summed = jnp.einsum(
        "bkij,bkjh->bih", tile_block, picked_rows, preferred_element_type=jnp.float32
    )
    row_half = lax.psum_scatter(
        summed.reshape(row_blocks * block_size, hidden_width),
        "rep",
        scatter_dimension=0,
        tiled=True,
    )
    hidden = jnp.maximum(row_half + shift_bias, 0.0)
    row_mean = jnp.mean(hidden, axis=1, keepdims=True)
    centered = hidden - row_mean
    row_var = jnp.mean(centered * centered, axis=1, keepdims=True)
    return (centered / jnp.sqrt(row_var + 1e-05) * norm_gain).astype(jnp.bfloat16)


def solution(mesh):
    in_specs = (
        P(("rows", "rep"), None),
        P(),
        P(),
        P(),
        P("rows", "rep", None, None, None),
        P("rows", "rep", None),
        P("rows", "rep"),
        P(),
    )
    out_specs = P(("rows", "rep"), None)
    return jax.shard_map(
        per_device, mesh=mesh, in_specs=in_specs, out_specs=out_specs, check_vma=False
    )
```

profile of v0, /device:TPU:1, one launch (start us, length us, event | category | flops | bytes accessed | tf_op | source)
XLA Modules:
  0.0 219.7 jit_solution(15019068501015475521)
XLA Ops:
  6.5 0.0 copy-start
  6.5 0.0 all-gather.2.cloned.1.call-start
  6.5 0.9 copy-done
  7.4 1.8 convolution_convert_fusion
  9.2 0.0 all-gather.2.cloned.1.call-update
  9.2 0.0 reduce-scatter.2.cloned.1.call-start
  9.3 0.7 constant_dynamic-slice_fusion
  10.0 1.0 select_reduce_fusion
  11.0 0.1 reshape.66
  11.1 0.7 iota_compare_fusion.1
  11.8 123.1 %all-gather.2.cloned.1.call-done = bf16[32768,256]{1,0:T(8,128)(2,1)} async-done(((bf16[512,256]{1,0:T(8,128)(2,1)}), bf16[32768,256]{1,0:T(8,128)(2,1)}) %all-gather.2.cloned.1.call-update) | async-done | bytes 16777232 | tf_op jit(solution)/shard_map/all_gather | solution.py:15
  134.9 26.7 %gather_fusion = bf16[704,128,256]{2,1,0:T(8,128)(2,1)} fusion(bf16[256,128,256]{2,1,0:T(8,128)(2,1)} %bitcast.20, s32[1024]{0:T(1024)S(1)} %pad_clamp_fusion), kind=kCustom, calls=%fused_computation | custom fusion | bytes 92277504 | tf_op jit(solution)/shard_map/gather | solution.py:24
  161.6 0.0 copy-start.1
  161.6 0.0 copy-start.2
  161.6 0.0 copy-start.3
  161.6 23.8 %fusion = f32[8,256,128,1]{1,2,3,0:T(8,128)} fusion(bf16[8,88,128,256]{3,2,1,0:T(8,128)(2,1)} %bitcast.21, pred[8,88]{1,0:T(8,128)(4,1)S(1)} %iota_compare_fusion.1, bf16[8,1,88,128,128]{4,3,2,1,0:T(8,128)(2,1)} %param.12), kind=kOutput, calls=%fused_computation.1 | convolution fusion | flops 5928648704 | bytes 70255296 | tf_op jit(solution)/shard_map/bkij,bkjh->bih/dot_general | solution.py:27
  185.4 0.0 reduce-scatter.2.cloned.1.call-update
  185.4 23.0 %reduce-scatter.2.cloned.1.call-done = f32[512,256]{1,0:T(8,128)} async-done(((f32[1024,256]{1,0:T(8,128)}), f32[512,256]{1,0:T(8,128)}) %reduce-scatter.2.cloned.1.call-update) | async-done | bytes 524304 | tf_op jit(solution)/shard_map/reduce_scatter | solution.py:30
  208.4 0.0 copy-done.2
  208.4 1.2 fusion.5
  209.6 1.3 multiply_reduce_fusion
  210.9 0.0 copy-done.3
  210.9 2.0 multiply_convert_fusion
  212.9 0.0 copy-done.1
  (4 shorter events, 0.0 us)
Async XLA Ops:
  6.5 0.9 copy-start
  6.5 128.4 %all-gather.2.cloned.1.call-start = ((), (), s32[]{:S(2)}) async-start(), calls=%async_computation.1 | async-start | bytes 17039360 | tf_op jit(solution)/shard_map/all_gather | solution.py:15
  9.2 199.2 %reduce-scatter.2.cloned.1.call-start = ((), (), s32[]{:S(2)}) async-start(), calls=%async_computation.2 | async-start | bytes 1572864 | tf_op jit(solution)/shard_map/reduce_scatter | solution.py:30
  161.6 51.2 %copy-start.1 = (bf16[512,128]{1,0:T(8,128)(2,1)S(1)}, bf16[512,128]{1,0:T(8,128)(2,1)}, u32[]{:S(2)}) copy-start(bf16[512,128]{1,0:T(8,128)(2,1)} %param.8) | copy-start | bytes 393220
  161.6 46.8 %copy-start.2 = (f32[256]{0:T(256)S(1)}, f32[256]{0:T(256)}, u32[]{:S(2)}) copy-start(f32[256]{0:T(256)} %param.10) | copy-start | bytes 3076
  161.6 49.3 %copy-start.3 = (f32[256]{0:T(256)S(1)}, f32[256]{0:T(256)}, u32[]{:S(2)}) copy-start(f32[256]{0:T(256)} %param.11) | copy-start | bytes 3076
Sparse Core Ops, SparseCore 0:
  9.3 125.5 all-gather.1
  185.6 22.8 reduce-scatter.1
where the time goes:
time: 220 us
  waiting for transfers between devices  146 us (66%)
  local copies, waits for them, and re-layouts  28.4 us (13%)
  matrix products  25.5 us (12%)
  between operations  13.5 us (6%)
  other arithmetic  6.19 us (3%)
    all_gather x1, waiting for transfers between devices, per_device(): panel_rows = lax.all_gather(projected, 'rows', axis=0, tiled=True)  123 us
    gather x1, local copies, waits for them, and re-layouts, per_device(): picked_rows = panel_blocks[positions]  26.7 us
    dot_general x1, matrix products, per_device(): jnp.einsum('bkij,bkjh->bih', tile_block, picked_rows, preferred_element_t...  23.8 us
    reduce_scatter x1, waiting for transfers between devices, per_device(): lax.psum_scatter(summed.reshape(row_blocks * block_size, hidden_width), '...  23 us
  transfers between devices with their start and end apart: 2, of which 2 were waited for; matrix products, arithmetic and copies ran while one was open for 1% of the time, Pallas kernels for 0%

commit v1 on v0

--- a/solution.py
+++ b/solution.py
@@ -2,6 +2,12 @@
 import jax.numpy as jnp
 from jax import lax
 from jax.sharding import PartitionSpec as P
+
+
+def spans_advance(local, axis_id, join_dim):
+    inter = jnp.stack(tuple((local for _ in range(jax.lax.axis_size(axis_id)))), 0)
+    odd = jax.lax.all_to_all(inter, axis_id, 0, 0)
+    return jnp.concatenate(odd, join_dim)
 
 
 def per_device(
@@ -12,7 +18,7 @@
     block_size = tile_values.shape[3]
     hidden_width = weight.shape[1]
     projected = jnp.dot(features, weight, preferred_element_type=jnp.float32).astype(jnp.bfloat16)
-    panel_rows = lax.all_gather(projected, "rows", axis=0, tiled=True)
+    panel_rows = spans_advance(projected, "rows", 0)
     set_blocks = panel_rows.shape[0] // block_size
     panel_blocks = panel_rows.reshape(set_blocks, block_size, hidden_width)
     order_mine = lax.dynamic_index_in_dim(block_order, lax.axis_index("rep"), 0, keepdims=False)

time: 220 us -> 339 us (1.54)
  waiting for transfers between devices: 146 us -> 250 us
  starting transfers between devices: 0.04 us -> 11.1 us
  local copies, waits for them, and re-layouts: 28.4 us -> 33.8 us
    all_to_all x0 -> x1, waiting for transfers between devices: none -> 216 us  [spans_advance(): odd = jax.lax.all_to_all(inter, axis_id, 0, 0)]
    all_gather x1 -> x0, waiting for transfers between devices: 123 us -> none  [per_device(): panel_rows = lax.all_gather(projected, 'rows', axis=0, tiled=True)]
    reduce_scatter x1, waiting for transfers between devices: 23 us -> 34.2 us  [per_device(): lax.psum_scatter(summed.reshape(row_blocks * block_size, hidden_width), '...]
    all_to_all x0 -> x1, starting transfers between devices: none -> 11 us  [spans_advance(): odd = jax.lax.all_to_all(inter, axis_id, 0, 0)]
    another operation x0 -> x1, local copies, waits for them, and re-layouts: none -> 6.05 us  [spans_advance(): jnp.stack(tuple((local for _ in range(jax.lax.axis_size(axis_id)))), 0)]
  transfers between devices with their start and end apart: 2 -> 2, of which waited for: 2 -> 2; matrix products, arithmetic and copies ran while one was open for 1% -> 0% of each run, Pallas kernels for 0% -> 0%
where the time goes in v1:
time: 339 us; the launch traced here: 338 us
  waiting for transfers between devices  250 us (74%)
  local copies, waits for them, and re-layouts  33.8 us (10%)
  matrix products  24.8 us (7%)
  between operations  13.5 us (4%)
  starting transfers between devices  11.1 us (3%)
  other arithmetic  4.85 us (1%)
    all_to_all x1, waiting for transfers between devices, spans_advance(): odd = jax.lax.all_to_all(inter, axis_id, 0, 0)  216 us
    reduce_scatter x1, waiting for transfers between devices, per_device(): lax.psum_scatter(summed.reshape(row_blocks * block_size, hidden_width), '...  34.2 us
    gather x1, local copies, waits for them, and re-layouts, per_device(): picked_rows = panel_blocks[positions]  26.7 us
    dot_general x1, matrix products, per_device(): jnp.einsum('bkij,bkjh->bih', tile_block, picked_rows, preferred_element_t...  23.8 us
    all_to_all x1, starting transfers between devices, spans_advance(): odd = jax.lax.all_to_all(inter, axis_id, 0, 0)  11 us
  transfers between devices with their start and end apart: 2, of which 2 were waited for; matrix products, arithmetic and copies ran while one was open for 0% of the time, Pallas kernels for 0%

profile of v1, /device:TPU:1, one launch (start us, length us, event | category | flops | bytes accessed | tf_op | source)
XLA Modules:
  0.0 338.3 jit_solution(6513841473250034604)
XLA Ops:
  6.5 0.0 copy-start
  6.5 0.0 copy-start.5
  6.5 0.0 copy-start.3
  6.5 0.0 copy-start.6
  6.5 0.9 copy-done
  7.4 1.0 convolution_convert_fusion
  8.5 6.1 %stack.2 = bf16[64,512,256]{2,1,0:T(8,128)(2,1)} broadcast(bf16[512,256]{1,0:T(8,128)(2,1)S(1)} %convolution_convert_fusion), dimensions={1,2} | broadcast | bytes 17039360 | tf_op jit(solution)/shard_map/stack | solution.py:8
  14.5 11.0 %all-to-all-start = ((bf16[64,512,256]{2,1,0:T(8,128)(2,1)}), bf16[64,512,256]{2,1,0:T(8,128)(2,1)}, u32[]{:S(2)}, u32[]{:S(2)}) async-start(bf16[64,512,256]{2,1,0:T(8,128)(2,1)} %stack.2), calls=%async_computation | async-start | bytes 33554432 | tf_op jit(solution)/shard_map/all_to_all | solution.py:9
  25.6 0.0 reduce-scatter.2.cloned.1.call-start
  25.6 0.0 copy-done.5
  25.6 0.0 copy-done.3
  25.7 0.3 select_reduce_fusion
  26.0 0.1 reshape.64
  26.1 0.0 copy-done.6
  26.1 0.1 iota_compare_fusion.1
  26.2 216.1 %all-to-all-done = bf16[64,512,256]{2,1,0:T(8,128)(2,1)} async-done(((bf16[64,512,256]{2,1,0:T(8,128)(2,1)}), bf16[64,512,256]{2,1,0:T(8,128)(2,1)}, u32[]{:S(2)}, u32[]{:S(2)}) %all-to-all-start) | async-done | bytes 16777248 | tf_op jit(solution)/shard_map/all_to_all | solution.py:9
  242.3 26.7 %gather_fusion = bf16[704,128,256]{2,1,0:T(8,128)(2,1)} fusion(bf16[256,128,256]{2,1,0:T(8,128)(2,1)} %bitcast.1, s32[1024]{0:T(1024)S(1)} %pad_clamp_fusion), kind=kCustom, calls=%fused_computation | custom fusion | bytes 92277504 | tf_op jit(solution)/shard_map/gather | solution.py:30
  269.0 0.0 copy-start.1
  269.0 0.0 copy-start.2
  269.0 0.0 copy-start.4
  269.0 23.8 %fusion = f32[8,256,128,1]{1,2,3,0:T(8,128)} fusion(bf16[8,88,128,256]{3,2,1,0:T(8,128)(2,1)} %bitcast.20, pred[8,88]{1,0:T(8,128)(4,1)S(1)} %iota_compare_fusion.1, bf16[8,1,88,128,128]{4,3,2,1,0:T(8,128)(2,1)} %param.12), kind=kOutput, calls=%fused_computation.1 | convolution fusion | flops 5928648704 | bytes 70255296 | tf_op jit(solution)/shard_map/bkij,bkjh->bih/dot_general | solution.py:33
  292.8 0.0 reduce-scatter.2.cloned.1.call-update
  292.8 34.2 %reduce-scatter.2.cloned.1.call-done = f32[512,256]{1,0:T(8,128)} async-done(((f32[1024,256]{1,0:T(8,128)}), f32[512,256]{1,0:T(8,128)}) %reduce-scatter.2.cloned.1.call-update) | async-done | bytes 524304 | tf_op jit(solution)/shard_map/reduce_scatter | solution.py:36
  327.0 0.0 copy-done.2
  327.0 1.2 fusion.5
  328.2 1.3 multiply_reduce_fusion
  329.5 0.0 copy-done.4
  329.5 2.0 multiply_convert_fusion
  331.5 0.0 copy-done.1
  (5 shorter events, 0.0 us)
Async XLA Ops:
  6.5 0.9 copy-start
  6.5 19.1 %copy-start.5 = (s32[2,256]{1,0:T(2,128)S(1)}, s32[2,256]{1,0:T(2,128)}, u32[]{:S(2)}) copy-start(s32[2,256]{1,0:T(2,128)} %param.15) | copy-start | bytes 6148
  6.5 19.1 %copy-start.3 = (s32[8,1,88]{2,1,0:T(1,128)S(1)}, s32[8,1,88]{2,1,0:T(1,128)}, u32[]{:S(2)}) copy-start(s32[8,1,88]{2,1,0:T(1,128)} %param.13) | copy-start | bytes 8452
  6.5 19.6 %copy-start.6 = (s32[8,1]{0,1:T(1,128)S(1)}, s32[8,1]{0,1:T(1,128)}, u32[]{:S(2)}) copy-start(s32[8,1]{0,1:T(1,128)} %param.14) | copy-start | bytes 100
  14.5 227.7 %all-to-all-start = ((bf16[64,512,256]{2,1,0:T(8,128)(2,1)}), bf16[64,512,256]{2,1,0:T(8,128)(2,1)}, u32[]{:S(2)}, u32[]{:S(2)}) async-start(bf16[64,512,256]{2,1,0:T(8,128)(2,1)} %stack.2), calls=%async_computation | async-start | bytes 33554432 | tf_op jit(solution)/shard_map/all_to_all | solution.py:9
  25.6 301.4 %reduce-scatter.2.cloned.1.call-start = ((), (), s32[]{:S(2)}) async-start(), calls=%async_computation.2 | async-start | bytes 1572864 | tf_op jit(solution)/shard_map/reduce_scatter | solution.py:36
  269.0 62.5 %copy-start.1 = (bf16[512,128]{1,0:T(8,128)(2,1)S(1)}, bf16[512,128]{1,0:T(8,128)(2,1)}, u32[]{:S(2)}) copy-start(bf16[512,128]{1,0:T(8,128)(2,1)} %param.8) | copy-start | bytes 393220
  269.0 58.0 %copy-start.2 = (f32[256]{0:T(256)S(1)}, f32[256]{0:T(256)}, u32[]{:S(2)}) copy-start(f32[256]{0:T(256)} %param.10) | copy-start | bytes 3076
  269.0 60.5 %copy-start.4 = (f32[256]{0:T(256)S(1)}, f32[256]{0:T(256)}, u32[]{:S(2)}) copy-start(f32[256]{0:T(256)} %param.11) | copy-start | bytes 3076
Sparse Core Ops, SparseCore 0:
  292.9 34.0 reduce-scatter.1
